TPU v7x, 32 devices: a whole 2x2x4 slice. The times are simulated.
32 devices in a mesh: row: 16 (over z, y, x), col: 2 (over core).
Axes of the slice: x: 2, y: 2, z: 4, core: 2. Of those that a mesh axis runs over, the one named last changes fastest.
Arguments:
- samples: bfloat16 [32768, 8192], P('row', 'col'), may hold values from -0.046875 to 0.046875
- targets: float32 [32768, 128], P('row'), may hold values from -6 to 6
- factor_inv: float32 [2, 4096, 4096], P('col', None, 'row'), may hold values from -1 to 1, as said below
Outputs:
- solution: float32 [8192, 128], P('col')
- residual: float32 [32768, 128], P('row')
Inputs may be any that keep to these rules, and one draw needn't show every extreme that they name: Each factor_inv[j] is lower triangular with a positive diagonal.
All inputs are finite; a program needn't handle non-finite values.
Results may differ from a plain program's by a relative error of at most 0.0039.
Values sent between devices are 32-bit elements; how exact they have to be, the bound alone decides.
A program may use at most 128 MiB of HBM per device.

v0:
```python
import jax
import jax.numpy as jnp
from jax import lax
from jax.sharding import PartitionSpec as P

ROUNDS = 3
ridge_weight = 0.5


def run_group(samples, residual, inverse, own_rows, offset, relaxation):
    solution = jnp.zeros((samples.shape[1], residual.shape[1]), jnp.float32)
    for sweep in range(ROUNDS):
        res16 = residual.astype(jnp.bfloat16)
        part_grad = jnp.einsum("rb,rk->bk", samples, res16, preferred_element_type=jnp.float32)
        own_solution = lax.dynamic_slice_in_dim(solution, offset, own_rows, 0)
        grad_own = (
            lax.psum_scatter(part_grad, "row", scatter_dimension=0, tiled=True)
            - ridge_weight * own_solution
        )
        term = jnp.dot(inverse, grad_own, precision=lax.Precision.HIGHEST)
        image = lax.psum(term, "row")
        update_own = jnp.einsum("bc,bk->ck", inverse, image, precision=lax.Precision.HIGHEST)
        update = lax.all_gather(update_own, "row", axis=0, tiled=True)
        solution = solution + relaxation * update
        change = jnp.dot(samples, update.astype(jnp.bfloat16), preferred_element_type=jnp.float32)
        residual = residual - relaxation * lax.psum(change, "col")
    return (solution, residual)


def per_device(samples, targets, factor_inv):
    inverse = factor_inv[0]
    own_rows = inverse.shape[1]
    offset = lax.axis_index("row") * own_rows
    relaxation = 1.0 / lax.axis_size("col")
    solution, residual = run_group(samples, targets, inverse, own_rows, offset, relaxation)
    return (solution, residual)


def solution(mesh):
    in_specs = (P("row", "col"), P("row", None), P("col", None, "row"))
    out_specs = (P("col", None), P("row", None))
    return jax.shard_map(
        per_device, mesh=mesh, in_specs=in_specs, out_specs=out_specs, check_vma=False
    )
```

profile of v0, /device:TPU:0, one launch (start us, length us, event | category | flops | bytes accessed | tf_op | source)
XLA Modules:
  0.0 985.5 jit_solution(3133331421541427131)
XLA Ops:
  7.2 0.0 reduce-scatter.4.cloned.1.call-start
  7.2 11.9 %fusion.23 = f32[4096,128]{1,0:T(8,128)} fusion(bf16[2048,4096]{1,0:T(8,128)(2,1)} %param.3, f32[2048,128]{1,0:T(8,128)} %param.4), kind=kOutput, calls=%fused_computation.31 | convolution fusion | flops 2147745792 | bytes 19922944 | tf_op jit(solution)/shard_map/rb,rk->bk/dot_general | solution.py:14
  19.1 0.0 all-reduce.7.cloned.1.call-start
  19.2 83.5 %reduce-scatter.4.cloned.1.call-done = f32[256,128]{1,0:T(8,128)} async-done(((f32[4096,128]{1,0:T(8,128)}), f32[256,128]{1,0:T(8,128)}) %reduce-scatter.4.cloned.1.call-update) | async-done | bytes 131088 | tf_op jit(solution)/shard_map/reduce_scatter | solution.py:17
  102.7 8.1 convolution_bitcast_fusion.4
  110.7 0.0 all-reduce.7.cloned.1.call-update
  110.8 0.0 all-gather.4.cloned.1.call-start
  110.8 123.0 %all-reduce.7.cloned.1.call-done = f32[4096,128]{0,1:T(8,128)} async-done(((f32[4096,128]{0,1:T(8,128)}), f32[4096,128]{0,1:T(8,128)}) %all-reduce.7.cloned.1.call-update) | async-done | bytes 2097168 | tf_op jit(solution)/shard_map/psum | solution.py:21
  233.9 5.6 fusion.9
  239.4 0.0 all-gather.4.cloned.1.call-update
  239.5 0.5 all-reduce.9.cloned.1.call-start
  240.0 60.7 %all-gather.4.cloned.1.call-done = f32[4096,128]{0,1:T(8,128)} async-done(((f32[256,128]{0,1:T(8,128)}), f32[4096,128]{0,1:T(8,128)}) %all-gather.4.cloned.1.call-update) | async-done | bytes 2097168 | tf_op jit(solution)/shard_map/all_gather | solution.py:23
  300.7 13.0 %convolution_bitcast_fusion.7 = f32[2048,128]{0,1:T(8,128)} fusion(bf16[2048,4096]{1,0:T(8,128)(2,1)} %param.3, f32[4096,128]{0,1:T(8,128)} %all-gather.4.cloned.1.call-done), kind=kOutput, calls=%fused_computation.16 | convolution fusion | flops 2148007936 | bytes 19922944 | tf_op jit(solution)/shard_map/dot_general | solution.py:25
  313.7 0.0 all-reduce.9.cloned.1.call-update
  313.8 0.0 reduce-scatter.6.cloned.1.call-start
  313.8 0.3 copy.5
  314.2 17.5 %all-reduce.9.cloned.1.call-done = f32[2048,128]{0,1:T(8,128)} async-done(((f32[2048,128]{0,1:T(8,128)}), f32[2048,128]{0,1:T(8,128)}) %all-reduce.9.cloned.1.call-update) | async-done | bytes 1048592 | tf_op jit(solution)/shard_map/psum | solution.py:26
  331.7 9.8 convolution_bitcast_fusion.1
  341.5 0.0 all-reduce.11.cloned.1.call-start
  341.6 1.5 copy-done
  343.1 1.5 broadcast_multiply_fusion
  344.6 78.9 %reduce-scatter.6.cloned.1.call-done = f32[256,128]{0,1:T(8,128)} async-done(((f32[4096,128]{0,1:T(8,128)}), f32[256,128]{0,1:T(8,128)}) %reduce-scatter.6.cloned.1.call-update) | async-done | bytes 131088 | tf_op jit(solution)/shard_map/reduce_scatter | solution.py:17
  423.5 7.9 convolution_bitcast_fusion.3
  431.4 0.0 all-reduce.11.cloned.1.call-update
  431.4 0.2 all-gather.6.cloned.1.call-start
  431.6 122.8 %all-reduce.11.cloned.1.call-done = f32[4096,128]{0,1:T(8,128)} async-done(((f32[4096,128]{0,1:T(8,128)}), f32[4096,128]{0,1:T(8,128)}) %all-reduce.11.cloned.1.call-update) | async-done | bytes 2097168 | tf_op jit(solution)/shard_map/psum | solution.py:21
  554.5 5.6 fusion.12
  560.1 0.0 all-reduce.13.cloned.1.call-start
  560.1 61.2 %all-gather.6.cloned.1.call-done = f32[4096,128]{0,1:T(8,128)} async-done(((f32[256,128]{0,1:T(8,128)}), f32[4096,128]{0,1:T(8,128)}) %all-gather.6.cloned.1.call-update) | async-done | bytes 2097168 | tf_op jit(solution)/shard_map/all_gather | solution.py:23
  621.3 13.0 %convolution_bitcast_fusion.6 = f32[2048,128]{0,1:T(8,128)} fusion(bf16[2048,4096]{1,0:T(8,128)(2,1)} %param.3, f32[4096,128]{0,1:T(8,128)} %all-gather.6.cloned.1.call-done), kind=kOutput, calls=%fused_computation.15 | convolution fusion | flops 2148007936 | bytes 19922944 | tf_op jit(solution)/shard_map/dot_general | solution.py:25
  634.4 0.0 reduce-scatter.8.cloned.1.call-start
  634.4 17.9 %all-reduce.13.cloned.1.call-done = f32[2048,128]{0,1:T(8,128)} async-done(((f32[2048,128]{0,1:T(8,128)}), f32[2048,128]{0,1:T(8,128)}) %all-reduce.13.cloned.1.call-update) | async-done | bytes 1048592 | tf_op jit(solution)/shard_map/psum | solution.py:26
  652.3 10.2 %convolution_bitcast_fusion = f32[4096,128]{0,1:T(8,128)} fusion(bf16[2048,4096]{1,0:T(8,128)(2,1)} %param.3, f32[2048,128]{0,1:T(8,128)} %all-reduce.13.cloned.1.call-done, f32[2048,128]{0,1:T(8,128)S(1)} %copy.5, f32[2048,128]{0,1:T(8,128)} %all-reduce.9.cloned.1.call-done), kind=kOutput, calls=%fused_computation | convolution fusion | flops 2148794368 | bytes 22020096 | tf_op jit(solution)/shard_map/rb,rk->bk/dot_general | solution.py:14
  662.5 0.3 all-reduce.15.cloned.1.call-start
  662.8 3.2 multiply_add_fusion.1
  665.9 78.6 %reduce-scatter.8.cloned.1.call-done = f32[256,128]{0,1:T(8,128)} async-done(((f32[4096,128]{0,1:T(8,128)}), f32[256,128]{0,1:T(8,128)}) %reduce-scatter.8.cloned.1.call-update) | async-done | bytes 131088 | tf_op jit(solution)/shard_map/reduce_scatter | solution.py:17
  744.5 7.9 convolution_bitcast_fusion.2
  752.5 0.0 all-gather.8.cloned.1.call-start
  752.6 122.8 %all-reduce.15.cloned.1.call-done = f32[4096,128]{0,1:T(8,128)} async-done(((f32[4096,128]{0,1:T(8,128)}), f32[4096,128]{0,1:T(8,128)}) %all-reduce.15.cloned.1.call-update) | async-done | bytes 2097168 | tf_op jit(solution)/shard_map/psum | solution.py:21
  875.4 5.6 fusion.15
  881.0 0.0 all-reduce.17.cloned.1.call-start
  881.0 61.2 %all-gather.8.cloned.1.call-done = f32[4096,128]{0,1:T(8,128)} async-done(((f32[256,128]{0,1:T(8,128)}), f32[4096,128]{0,1:T(8,128)}) %all-gather.8.cloned.1.call-update) | async-done | bytes 2097168 | tf_op jit(solution)/shard_map/all_gather | solution.py:23
  942.2 13.2 %convolution_bitcast_fusion.5 = f32[2048,128]{0,1:T(8,128)} fusion(bf16[2048,4096]{1,0:T(8,128)(2,1)} %param.3, f32[4096,128]{0,1:T(8,128)} %all-gather.8.cloned.1.call-done), kind=kOutput, calls=%fused_computation.14 | convolution fusion | flops 2148007936 | bytes 19922944 | tf_op jit(solution)/shard_map/dot_general | solution.py:25
  955.4 3.1 multiply_add_fusion
  958.6 3.3 copy.6
  961.9 11.5 %all-reduce.17.cloned.1.call-done = f32[2048,128]{0,1:T(8,128)} async-done(((f32[2048,128]{0,1:T(8,128)}), f32[2048,128]{0,1:T(8,128)}) %all-reduce.17.cloned.1.call-update) | async-done | bytes 1048592 | tf_op jit(solution)/shard_map/psum | solution.py:26
  973.4 2.5 multiply_subtract_fusion
  975.9 2.5 copy.7
  (17 shorter events, 0.1 us)
Async XLA Ops:
  7.2 95.5 %reduce-scatter.4.cloned.1.call-start = ((), (), s32[]{:S(2)}) async-start(), calls=%async_computation.3 | async-start | bytes 2228224 | tf_op jit(solution)/shard_map/reduce_scatter | solution.py:17
  19.1 214.7 %all-reduce.7.cloned.1.call-start = ((), (), s32[]{:S(2)}) async-start(), calls=%async_computation.4 | async-start | bytes 4194304 | tf_op jit(solution)/shard_map/psum | solution.py:21
  110.8 190.0 %all-gather.4.cloned.1.call-start = ((), (), s32[]{:S(2)}) async-start(), calls=%async_computation.5 | async-start | bytes 2228224 | tf_op jit(solution)/shard_map/all_gather | solution.py:23
  239.5 74.4 %copy-start.4 = (f32[2048,128]{1,0:T(8,128)S(1)}, f32[2048,128]{1,0:T(8,128)}, u32[]{:S(2)}) copy-start(f32[2048,128]{1,0:T(8,128)} %param.4) | copy-start | bytes 3145732
  239.5 92.2 %all-reduce.9.cloned.1.call-start = ((), (), s32[]{:S(2)}) async-start(), calls=%async_computation.6 | async-start | bytes 2097152 | tf_op jit(solution)/shard_map/psum | solution.py:26
  313.8 109.7 %reduce-scatter.6.cloned.1.call-start = ((), (), s32[]{:S(2)}) async-start(), calls=%async_computation.7 | async-start | bytes 2228224 | tf_op jit(solution)/shard_map/reduce_scatter | solution.py:17
  341.5 1.6 copy-start
  341.5 213.0 %all-reduce.11.cloned.1.call-start = ((), (), s32[]{:S(2)}) async-start(), calls=%async_computation.8 | async-start | bytes 4194304 | tf_op jit(solution)/shard_map/psum | solution.py:21
  431.4 189.9 %all-gather.6.cloned.1.call-start = ((), (), s32[]{:S(2)}) async-start(), calls=%async_computation.9 | async-start | bytes 2228224 | tf_op jit(solution)/shard_map/all_gather | solution.py:23
  560.1 92.3 %all-reduce.13.cloned.1.call-start = ((), (), s32[]{:S(2)}) async-start(), calls=%async_computation.10 | async-start | bytes 2097152 | tf_op jit(solution)/shard_map/psum | solution.py:26
  634.4 110.2 %reduce-scatter.8.cloned.1.call-start = ((), (), s32[]{:S(2)}) async-start(), calls=%async_computation.11 | async-start | bytes 2228224 | tf_op jit(solution)/shard_map/reduce_scatter | solution.py:17
  662.5 212.9 %all-reduce.15.cloned.1.call-start = ((), (), s32[]{:S(2)}) async-start(), calls=%async_computation.12 | async-start | bytes 4194304 | tf_op jit(solution)/shard_map/psum | solution.py:21
  752.5 189.7 %all-gather.8.cloned.1.call-start = ((), (), s32[]{:S(2)}) async-start(), calls=%async_computation.13 | async-start | bytes 2228224 | tf_op jit(solution)/shard_map/all_gather | solution.py:23
  881.0 92.4 %all-reduce.17.cloned.1.call-start = ((), (), s32[]{:S(2)}) async-start(), calls=%async_computation.14 | async-start | bytes 2097152 | tf_op jit(solution)/shard_map/psum | solution.py:26
  942.2 13.2 %copy-start.2 = (f32[4096,128]{0,1:T(8,128)S(1)}, f32[4096,128]{0,1:T(8,128)}, u32[]{:S(2)}) copy-start(f32[4096,128]{0,1:T(8,128)} %multiply_add_fusion.1) | copy-start | bytes 6291460
  958.6 14.8 %copy-start.1 = (f32[2048,128]{0,1:T(8,128)S(1)}, f32[2048,128]{0,1:T(8,128)}, u32[]{:S(2)}) copy-start(f32[2048,128]{0,1:T(8,128)} %all-reduce.9.cloned.1.call-done) | copy-start | bytes 3145732
  958.6 14.8 %copy-start.3 = (f32[2048,128]{0,1:T(8,128)S(1)}, f32[2048,128]{0,1:T(8,128)}, u32[]{:S(2)}) copy-start(f32[2048,128]{0,1:T(8,128)} %all-reduce.13.cloned.1.call-done) | copy-start | bytes 3145732
Sparse Core Ops, SparseCore 0:
  19.3 83.3 reduce-scatter.3
  110.9 122.9 all-reduce.6
  239.6 61.0 all-gather.3
  313.9 17.7 all-reduce.8
  341.6 81.7 reduce-scatter.5
  431.5 122.8 all-reduce.10
  560.2 61.0 all-gather.5
  634.5 17.7 all-reduce.12
  662.6 81.8 reduce-scatter.7
  752.6 122.7 all-reduce.14
  881.1 61.0 all-gather.7
  955.6 17.7 all-reduce.16
where the time goes:
time: 994 us; the launch traced here: 986 us
  waiting for transfers between devices  840 us (85%)
  matrix products  112 us (11%)
  between operations  14.5 us (1%)
  other arithmetic  10.3 us (1%)
    psum x3, waiting for transfers between devices, run_group(): image = lax.psum(term, 'row')  369 us
    reduce_scatter x3, waiting for transfers between devices, run_group(): lax.psum_scatter(part_grad, 'row', scatter_dimension=0, tiled=True)  241 us
    all_gather x3, waiting for transfers between devices, run_group(): update = lax.all_gather(update_own, 'row', axis=0, tiled=True)  183 us
    psum x3, waiting for transfers between devices, run_group(): residual = residual - relaxation * lax.psum(change, 'col')  46.9 us
    dot_general x3, matrix products, run_group(): jnp.dot(samples, update.astype(jnp.bfloat16), preferred_element_type=jnp....  39.2 us
    dot_general x3, matrix products, run_group(): jnp.einsum('rb,rk->bk', samples, res16, preferred_element_type=jnp.float32)  31.9 us
    dot_general x3, matrix products, run_group(): term = jnp.dot(inverse, grad_own, precision=lax.Precision.HIGHEST)  23.9 us
  transfers between devices with their start and end apart: 12, of which 12 were waited for; matrix products, arithmetic and copies ran while one was open for 1% of the time, Pallas kernels for 0%

commit v1 on v0

--- a/solution.py
+++ b/solution.py
@@ -5,6 +5,22 @@
 
 ROUNDS = 3
 ridge_weight = 0.5
+
+
+def drive_heads(base_x, shard_axis):
+    t1 = lax.axis_size(shard_axis)
+    block_last, v1, x_new = (t1, lax.axis_index(shard_axis), base_x.shape[0])
+    pages = list(map(lambda s: (s, (s + 1) % block_last), range(block_last)))
+    earlier = jnp.zeros((*base_x.shape[:0], block_last * x_new, *base_x.shape[1:]), base_x.dtype)
+    h_now = base_x
+    i0 = 0
+    while i0 < block_last:
+        found_now = (v1 - i0) % block_last
+        earlier = lax.dynamic_update_slice_in_dim(earlier, h_now, found_now * x_new, axis=0)
+        if i0 < block_last - 1:
+            h_now = lax.ppermute(h_now, shard_axis, pages)
+        i0 += 1
+    return earlier
 
 
 def run_group(samples, residual, inverse, own_rows, offset, relaxation):
@@ -20,7 +36,7 @@
         term = jnp.dot(inverse, grad_own, precision=lax.Precision.HIGHEST)
         image = lax.psum(term, "row")
         update_own = jnp.einsum("bc,bk->ck", inverse, image, precision=lax.Precision.HIGHEST)
-        update = lax.all_gather(update_own, "row", axis=0, tiled=True)
+        update = drive_heads(update_own, "row")
         solution = solution + relaxation * update
         change = jnp.dot(samples, update.astype(jnp.bfloat16), preferred_element_type=jnp.float32)
         residual = residual - relaxation * lax.psum(change, "col")

time: 994 us -> 1210 us (1.22)
  waiting for transfers between devices: 840 us -> 1010 us
  local copies, waits for them, and re-layouts: 7.7 us -> 42 us
    ppermute x0 -> x45, waiting for transfers between devices: none -> 353 us  [drive_heads(): h_now = lax.ppermute(h_now, shard_axis, pages)]
    all_gather x3 -> x0, waiting for transfers between devices: 183 us -> none  [run_group(): update = lax.all_gather(update_own, 'row', axis=0, tiled=True)]
    ppermute x0 -> x45, local copies, waits for them, and re-layouts: none -> 22.1 us  [drive_heads(): h_now = lax.ppermute(h_now, shard_axis, pages)]
  transfers between devices with their start and end apart: 12 -> 54, of which waited for: 12 -> 54; matrix products, arithmetic and copies ran while one was open for 1% -> 4% of each run, Pallas kernels for 0% -> 0%
where the time goes in v1:
time: 1210 us; the launch traced here: 1200 us
  waiting for transfers between devices  1010 us (83%)
  matrix products  117 us (10%)
  local copies, waits for them, and re-layouts  42 us (3%)
  between operations  15.3 us (1%)
    psum x3, waiting for transfers between devices, run_group(): image = lax.psum(term, 'row')  369 us
    ppermute x45, waiting for transfers between devices, drive_heads(): h_now = lax.ppermute(h_now, shard_axis, pages)  353 us
    reduce_scatter x3, waiting for transfers between devices, run_group(): lax.psum_scatter(part_grad, 'row', scatter_dimension=0, tiled=True)  243 us
    psum x3, waiting for transfers between devices, run_group(): residual = residual - relaxation * lax.psum(change, 'col')  41.9 us
    dot_general x3, matrix products, run_group(): jnp.einsum('rb,rk->bk', samples, res16, preferred_element_type=jnp.float32)  40.4 us
    dot_general x3, matrix products, run_group(): jnp.dot(samples, update.astype(jnp.bfloat16), preferred_element_type=jnp....  37.9 us
    dot_general x3, matrix products, run_group(): term = jnp.dot(inverse, grad_own, precision=lax.Precision.HIGHEST)  24.3 us
  transfers between devices with their start and end apart: 54, of which 54 were waited for; matrix products, arithmetic and copies ran while one was open for 4% of the time, Pallas kernels for 0%

profile of v1, /device:TPU:0, one launch (start us, length us, event | category | flops | bytes accessed | tf_op | source)
XLA Modules:
  0.0 1197.5 jit_solution(12678791152060580786)
XLA Ops:
  7.2 11.9 fusion.23
  19.2 83.5 %reduce-scatter.4.cloned.1.call-done = f32[256,128]{1,0:T(8,128)} async-done(((f32[4096,128]{1,0:T(8,128)}), f32[256,128]{1,0:T(8,128)}) %reduce-scatter.4.cloned.1.call-update) | async-done | bytes 131088 | tf_op jit(solution)/shard_map/reduce_scatter | solution.py:33
  102.7 8.1 convolution_bitcast_fusion.4
  110.8 123.0 %all-reduce.7.cloned.1.call-done = f32[4096,128]{0,1:T(8,128)} async-done(((f32[4096,128]{0,1:T(8,128)}), f32[4096,128]{0,1:T(8,128)}) %all-reduce.7.cloned.1.call-update) | async-done | bytes 2097168 | tf_op jit(solution)/shard_map/psum | solution.py:37
  247.9 8.6 collective-permute-done.1
  256.5 8.6 collective-permute-done.2
  265.0 8.6 collective-permute-done.3
  273.6 8.6 collective-permute-done.4
  282.2 8.9 collective-permute-done.5
  291.1 9.7 collective-permute-done.6
  301.8 8.1 collective-permute-done.7
  310.2 8.3 collective-permute-done.8
  318.7 8.3 collective-permute-done.9
  327.3 8.3 collective-permute-done.10
  335.8 8.3 collective-permute-done.11
  344.4 9.0 collective-permute-done.12
  353.7 8.3 collective-permute-done.13
  362.1 8.4 collective-permute-done.14
  370.7 12.4 %convolution_bitcast_fusion.7 = f32[2048,128]{0,1:T(8,128)} fusion(bf16[2048,4096]{1,0:T(8,128)(2,1)} %param.3, f32[4096,128]{1,0:T(8,128)S(1)} %constant_dynamic-update-slice_fusion.32), kind=kOutput, calls=%fused_computation.16 | convolution fusion | flops 2148007936 | bytes 19922944 | tf_op jit(solution)/shard_map/dot_general | solution.py:41
  384.7 14.0 %all-reduce.9.cloned.1.call-done = f32[2048,128]{0,1:T(8,128)} async-done(((f32[2048,128]{0,1:T(8,128)}), f32[2048,128]{0,1:T(8,128)}) %all-reduce.9.cloned.1.call-update) | async-done | bytes 1048592 | tf_op jit(solution)/shard_map/psum | solution.py:42
  398.7 14.0 %convolution_bitcast_fusion.1 = f32[4096,128]{1,0:T(8,128)} fusion(bf16[2048,4096]{1,0:T(8,128)(2,1)} %param.3, f32[2048,128]{0,1:T(8,128)S(1)} %copy.21, f32[2048,128]{0,1:T(8,128)} %all-reduce.9.cloned.1.call-done), kind=kOutput, calls=%fused_computation.1 | convolution fusion | flops 2148270080 | bytes 20971520 | tf_op jit(solution)/shard_map/rb,rk->bk/dot_general | solution.py:30
  414.3 80.4 %reduce-scatter.6.cloned.1.call-done = f32[256,128]{1,0:T(8,128)} async-done(((f32[4096,128]{1,0:T(8,128)}), f32[256,128]{1,0:T(8,128)}) %reduce-scatter.6.cloned.1.call-update) | async-done | bytes 131088 | tf_op jit(solution)/shard_map/reduce_scatter | solution.py:33
  494.7 8.1 convolution_bitcast_fusion.3
  503.1 123.1 %all-reduce.11.cloned.1.call-done = f32[4096,128]{0,1:T(8,128)} async-done(((f32[4096,128]{0,1:T(8,128)}), f32[4096,128]{0,1:T(8,128)}) %all-reduce.11.cloned.1.call-update) | async-done | bytes 2097168 | tf_op jit(solution)/shard_map/psum | solution.py:37
  640.9 7.9 collective-permute-done.16
  649.5 7.9 collective-permute-done.17
  658.1 7.9 collective-permute-done.18
  666.6 7.9 collective-permute-done.19
  674.5 8.9 collective-permute-done.20
  683.4 9.8 collective-permute-done.21
  764.7 13.0 %convolution_bitcast_fusion.6 = f32[2048,128]{0,1:T(8,128)} fusion(bf16[2048,4096]{1,0:T(8,128)(2,1)} %param.3, f32[4096,128]{1,0:T(8,128)} %constant_dynamic-update-slice_fusion.16), kind=kOutput, calls=%fused_computation.15 | convolution fusion | flops 2148007936 | bytes 19922944 | tf_op jit(solution)/shard_map/dot_general | solution.py:41
  778.0 15.4 %all-reduce.13.cloned.1.call-done = f32[2048,128]{0,1:T(8,128)} async-done(((f32[2048,128]{0,1:T(8,128)}), f32[2048,128]{0,1:T(8,128)}) %all-reduce.13.cloned.1.call-update) | async-done | bytes 1048592 | tf_op jit(solution)/shard_map/psum | solution.py:42
  793.4 14.4 %convolution_bitcast_fusion = f32[4096,128]{1,0:T(8,128)} fusion(bf16[2048,4096]{1,0:T(8,128)(2,1)} %param.3, f32[2048,128]{0,1:T(8,128)} %all-reduce.13.cloned.1.call-done, f32[2048,128]{0,1:T(8,128)S(1)} %copy.21, f32[2048,128]{0,1:T(8,128)} %all-reduce.9.cloned.1.call-done), kind=kOutput, calls=%fused_computation | convolution fusion | flops 2148794368 | bytes 22020096 | tf_op jit(solution)/shard_map/rb,rk->bk/dot_general | solution.py:30
  811.0 78.7 %reduce-scatter.8.cloned.1.call-done = f32[256,128]{1,0:T(8,128)} async-done(((f32[4096,128]{1,0:T(8,128)}), f32[256,128]{1,0:T(8,128)}) %reduce-scatter.8.cloned.1.call-update) | async-done | bytes 131088 | tf_op jit(solution)/shard_map/reduce_scatter | solution.py:33
  889.7 8.2 convolution_bitcast_fusion.2
  898.2 123.0 %all-reduce.15.cloned.1.call-done = f32[4096,128]{0,1:T(8,128)} async-done(((f32[4096,128]{0,1:T(8,128)}), f32[4096,128]{0,1:T(8,128)}) %all-reduce.15.cloned.1.call-update) | async-done | bytes 2097168 | tf_op jit(solution)/shard_map/psum | solution.py:37
  1035.8 7.9 collective-permute-done.31
  1044.4 7.9 collective-permute-done.32
  1052.3 8.6 collective-permute-done.33
  1060.9 8.6 collective-permute-done.34
  1069.5 8.9 collective-permute-done.35
  1078.4 9.8 collective-permute-done.36
  1089.5 7.8 collective-permute-done.37
  1116.0 7.7 collective-permute-done.40
  1141.6 8.4 collective-permute-done.43
  1151.1 7.7 collective-permute-done.44
  1159.0 12.4 %convolution_bitcast_fusion.5 = f32[2048,128]{0,1:T(8,128)} fusion(bf16[2048,4096]{1,0:T(8,128)(2,1)} %param.3, f32[4096,128]{1,0:T(8,128)S(1)} %constant_dynamic-update-slice_fusion), kind=kOutput, calls=%fused_computation.14 | convolution fusion | flops 2148007936 | bytes 19922944 | tf_op jit(solution)/shard_map/dot_general | solution.py:41
  1174.5 12.5 %all-reduce.17.cloned.1.call-done = f32[2048,128]{0,1:T(8,128)} async-done(((f32[2048,128]{0,1:T(8,128)}), f32[2048,128]{0,1:T(8,128)}) %all-reduce.17.cloned.1.call-update) | async-done | bytes 1048592 | tf_op jit(solution)/shard_map/psum | solution.py:42
  (210 shorter events, 172.1 us)
Async XLA Ops:
  7.2 95.5 %reduce-scatter.4.cloned.1.call-start = ((), (), s32[]{:S(2)}) async-start(), calls=%async_computation.3 | async-start | bytes 2228224 | tf_op jit(solution)/shard_map/reduce_scatter | solution.py:33
  19.2 214.7 %all-reduce.7.cloned.1.call-start = ((), (), s32[]{:S(2)}) async-start(), calls=%async_computation.4 | async-start | bytes 4194304 | tf_op jit(solution)/shard_map/psum | solution.py:37
  110.8 287.9 %all-reduce.9.cloned.1.call-start = ((), (), s32[]{:S(2)}) async-start(), calls=%async_computation.5 | async-start | bytes 2097152 | tf_op jit(solution)/shard_map/psum | solution.py:42
  238.8 9.1 collective-permute-start
  247.9 8.6 collective-permute-start.1
  256.5 8.6 collective-permute-start.2
  265.0 8.6 collective-permute-start.3
  273.6 8.6 collective-permute-start.4
  282.2 8.9 collective-permute-start.5
  291.1 9.7 collective-permute-start.6
  300.8 9.1 collective-permute-start.7
  309.9 8.6 collective-permute-start.8
  318.5 8.6 collective-permute-start.9
  327.0 8.6 collective-permute-start.10
  335.6 8.6 collective-permute-start.11
  344.2 9.2 collective-permute-start.12
  353.4 8.6 collective-permute-start.13
  362.0 8.6 collective-permute-start.14
  383.1 111.6 %reduce-scatter.6.cloned.1.call-start = ((), (), s32[]{:S(2)}) async-start(), calls=%async_computation.6 | async-start | bytes 2228224 | tf_op jit(solution)/shard_map/reduce_scatter | solution.py:33
  412.8 213.5 %all-reduce.11.cloned.1.call-start = ((), (), s32[]{:S(2)}) async-start(), calls=%async_computation.7 | async-start | bytes 4194304 | tf_op jit(solution)/shard_map/psum | solution.py:37
  502.9 290.5 %all-reduce.13.cloned.1.call-start = ((), (), s32[]{:S(2)}) async-start(), calls=%async_computation.8 | async-start | bytes 2097152 | tf_op jit(solution)/shard_map/psum | solution.py:42
  631.2 9.1 collective-permute-start.15
  640.3 8.6 collective-permute-start.16
  666.0 8.6 collective-permute-start.19
  674.5 8.9 collective-permute-start.20
  683.4 9.8 collective-permute-start.21
  693.3 9.1 collective-permute-start.22
  702.4 8.7 collective-permute-start.23
  711.1 8.9 collective-permute-start.24
  719.9 8.9 collective-permute-start.25
  728.8 8.8 collective-permute-start.26
  737.6 8.9 collective-permute-start.27
  746.5 8.7 collective-permute-start.28
  755.1 8.8 collective-permute-start.29
  777.7 112.0 %reduce-scatter.8.cloned.1.call-start = ((), (), s32[]{:S(2)}) async-start(), calls=%async_computation.9 | async-start | bytes 2228224 | tf_op jit(solution)/shard_map/reduce_scatter | solution.py:33
  807.8 213.4 %all-reduce.15.cloned.1.call-start = ((), (), s32[]{:S(2)}) async-start(), calls=%async_computation.10 | async-start | bytes 4194304 | tf_op jit(solution)/shard_map/psum | solution.py:37
  897.9 289.1 %all-reduce.17.cloned.1.call-start = ((), (), s32[]{:S(2)}) async-start(), calls=%async_computation.11 | async-start | bytes 2097152 | tf_op jit(solution)/shard_map/psum | solution.py:42
  1026.1 9.1 collective-permute-start.30
  1069.5 8.9 collective-permute-start.35
  1078.4 9.8 collective-permute-start.36
  1088.2 9.1 collective-permute-start.37
  1097.3 8.7 collective-permute-start.38
  1106.0 8.9 collective-permute-start.39
  1114.9 8.9 collective-permute-start.40
  1123.8 8.8 collective-permute-start.41
  1132.5 8.9 collective-permute-start.42
  1141.4 8.7 collective-permute-start.43
  1150.1 8.8 collective-permute-start.44
  (18 other events, 191.0 us)
Sparse Core Ops, SparseCore 0:
  19.3 83.3 reduce-scatter.3
  110.9 122.9 all-reduce.6
  383.2 15.4 all-reduce.8
  412.9 81.7 reduce-scatter.5
  503.0 123.1 all-reduce.10
  777.9 15.4 all-reduce.12
  807.9 81.7 reduce-scatter.7
  898.0 123.0 all-reduce.14
  1171.5 15.4 all-reduce.16
